TPU v7x, 128 devices: a whole 4x4x4 slice. The times are simulated.
128 devices in a mesh: row: 8 (over x, y_lo), col: 8 (over z, y_hi), depth: 2 (over core).
Axes of the slice: x: 4, y: 4 (y_hi: 2, y_lo: 2; y = y_hi * 2 + y_lo), z: 4, core: 2. Of those that a mesh axis runs over, the one named last changes fastest.
Arguments:
- amplitudes: bfloat16 [20480, 20480], P('row', 'col'), may hold values from -0.109375 to 0.109375
- coulomb_vertex: bfloat16 [256, 20480], P('depth', ('row', 'col')), may hold values from -1.5 to 1.5
Outputs:
- cycle_residual: bfloat16 [20480, 20480], P('row', ('col', 'depth'))
- structure_factor: float32 [256], P('depth')
All inputs are finite; a program needn't handle non-finite values.
Results may differ from a plain program's by a relative error of at most 0.0057.
Values may be sent and summed in bfloat16 or wider, within the bound.
No kernel may reach another device: no remote copies, remote signals or barrier semaphores. Data moves between devices by JAX's collectives and lax.ppermute only.
A program may use at most 128 MiB of HBM per device.

v0:
```python
import jax
import jax.numpy as jnp
from jax import lax
from jax.sharding import PartitionSpec as P


def broadcast(array, axis, root):
    mine = lax.axis_index(axis) == root
    return lax.psum(jnp.where(mine, array, jnp.zeros_like(array)), axis)


def body(amplitudes, coulomb_vertex):
    row_index = lax.axis_index("row")
    col_index = lax.axis_index("col")
    block_width = amplitudes.shape[0]
    on_diagonal = (row_index == col_index).astype(jnp.float32)
    vertex_rows = lax.all_gather(coulomb_vertex, "col", axis=1, tiled=True)
    vertex_cols = broadcast(vertex_rows, "row", col_index)
    dressing = jnp.dot(vertex_rows, amplitudes, preferred_element_type=jnp.float32)
    factor_part = jnp.sum(dressing * vertex_cols.astype(jnp.float32), axis=1)
    structure_factor = lax.psum(factor_part, ("row", "col"))
    dressed_term = dressing + on_diagonal * vertex_rows.astype(jnp.float32)
    dressed_part = lax.psum_scatter(dressed_term, "row", scatter_dimension=1, tiled=True)
    dressed = dressed_part.astype(jnp.bfloat16)
    everything = lax.all_gather(dressed, ("row", "col"), axis=1, tiled=True)
    fields_here = everything.shape[0]
    grid_side = lax.axis_size("row")
    ordered = everything.reshape(fields_here, grid_side, grid_side, dressed.shape[1])
    ordered = jnp.transpose(ordered, (0, 2, 1, 3)).reshape(
        fields_here, grid_side * grid_side * dressed.shape[1]
    )
    dressed_cols = lax.dynamic_slice_in_dim(ordered, col_index * block_width, block_width, 1)
    dressed_rows = lax.dynamic_slice_in_dim(ordered, row_index * block_width, block_width, 1)
    cols_all = lax.all_to_all(dressed_cols, "depth", split_axis=1, concat_axis=0, tiled=True)
    rows_all = lax.all_gather(dressed_rows, "depth", axis=0, tiled=True)
    product = lax.dot_general(
        rows_all, cols_all, (((0,), (0,)), ((), ())), preferred_element_type=jnp.float32
    )
    cycle_residual = product.astype(jnp.bfloat16)
    return (cycle_residual, structure_factor)


def solution(mesh):
    return jax.shard_map(
        body,
        mesh=mesh,
        in_specs=(P("row", "col"), P("depth", ("row", "col"))),
        out_specs=(P("row", ("col", "depth")), P("depth")),
        check_vma=False,
    )
```

profile of v0, /device:TPU:1, one launch (start us, length us, event | category | flops | bytes accessed | tf_op | source)
XLA Modules:
  0.0 711.8 jit_solution(17845553352122211983)
XLA Ops:
  7.2 0.0 all-reduce.2.cloned.1.call-start
  7.2 33.1 %all_gather.9 = bf16[128,2560]{0,1:T(8,128)(2,1)S(1)} all-gather(bf16[128,320]{0,1:T(8,128)(2,1)} %param.3), channel_id=1, replica_groups=mesh['row'=8,'col'=8,'depth'=2] {'col'}, dimensions={1}, use_global_device_ids=true | all-gather | bytes 737280 | tf_op jit(solution)/shard_map/all_gather | solution.py:17
  40.3 0.2 copy.17
  40.6 0.9 broadcast_select_fusion
  41.5 0.0 all-reduce.2.cloned.1.call-update
  41.5 0.0 reduce-scatter.4.cloned.1.call-start
  41.5 77.2 %all-reduce.2.cloned.1.call-done = bf16[128,2560]{1,0:T(8,128)(2,1)} async-done(((bf16[128,2560]{1,0:T(8,128)(2,1)}), bf16[128,2560]{1,0:T(8,128)(2,1)}) %all-reduce.2.cloned.1.call-update) | async-done | bytes 655376 | tf_op jit(solution)/shard_map/psum | solution.py:9
  118.7 6.9 multiply_reduce_fusion
  125.6 1.5 copy.22
  127.1 0.0 reduce-scatter.4.cloned.1.call-update
  127.1 0.0 all-gather.3.cloned.1.call-start
  127.1 42.3 %reduce-scatter.4.cloned.1.call-done = f32[320,128]{1,0:T(8,128)} async-done(((f32[2560,128]{1,0:T(8,128)}), f32[320,128]{1,0:T(8,128)}) %reduce-scatter.4.cloned.1.call-update) | async-done | bytes 163856
  169.5 1.6 bitcast_convert_fusion
  171.0 0.0 all-gather.3.cloned.1.call-update
  171.1 0.0 all-gather.5.cloned.1.call-start
  171.1 301.0 %all-gather.3.cloned.1.call-done = bf16[128,20480]{0,1:T(8,128)(2,1)} async-done(((bf16[128,320]{0,1:T(8,128)(2,1)}), bf16[128,20480]{0,1:T(8,128)(2,1)}) %all-gather.3.cloned.1.call-update) | async-done | bytes 5242896 | tf_op jit(solution)/shard_map/all_gather | solution.py:25
  472.2 2.9 copy.19
  475.1 0.9 constant_dynamic-slice_fusion
  476.0 0.0 all-gather.5.cloned.1.call-update
  476.1 148.3 %psum.15 = f32[128]{0:T(128)} all-reduce(f32[128]{0:T(128)S(1)} %get-tuple-element.4), channel_id=1, replica_groups=mesh['row'=8,'col'=8,'depth'=2] {'row','col'}, use_global_device_ids=true, to_apply=%region_3.4 | all-reduce | flops 128 | bytes 1024 | tf_op jit(solution)/shard_map/psum | solution.py:21
  624.3 74.7 %all_to_all.19 = bf16[128,2,1280]{0,2,1:T(8,128)(2,1)S(1)} all-to-all(bf16[128,2,1280]{0,2,1:T(8,128)(2,1)S(1)} %bitcast.19), channel_id=1, replica_groups=mesh['row'=8,'col'=8,'depth'=2] {'depth'}, dimensions={1} | all-to-all | bytes 1310720 | tf_op jit(solution)/shard_map/all_to_all | solution.py:34
  699.0 0.2 copy.20
  699.3 0.0 all-gather.5.cloned.1.call-done
  699.3 6.0 convolution_convert_fusion
Async XLA Ops:
  7.2 111.5 %all-reduce.2.cloned.1.call-start = ((), (), s32[]{:S(2)}) async-start(), calls=%async_computation.4 | async-start | bytes 1310720 | tf_op jit(solution)/shard_map/psum | solution.py:9
  41.5 128.0 %reduce-scatter.4.cloned.1.call-start = ((), (), s32[]{:S(2)}) async-start(), calls=%async_computation.5 | async-start | bytes 1474560
  127.1 345.1 %all-gather.3.cloned.1.call-start = ((), (), s32[]{:S(2)}) async-start(), calls=%async_computation.2 | async-start | bytes 5324800 | tf_op jit(solution)/shard_map/all_gather | solution.py:25
  171.1 528.3 %all-gather.5.cloned.1.call-start = ((), (), s32[]{:S(2)}) async-start(), calls=%async_computation.3 | async-start | bytes 1966080 | tf_op jit(solution)/shard_map/all_gather | solution.py:35
Sparse Core Ops, SparseCore 0:
  41.6 77.0 all-reduce.1
  127.2 42.2 reduce-scatter.3
  171.7 300.4 all-gather.2
  476.2 51.9 all-gather.4
where the time goes:
time: 712 us
  waiting for transfers between devices  421 us (59%)
  blocking collectives  256 us (36%)
  between operations  13.8 us (2%)
  matrix products  12.9 us (2%)
    all_gather x1, waiting for transfers between devices, body(): everything = lax.all_gather(dressed, ('row', 'col'), axis=1, tiled=True)  301 us
    psum x1, blocking collectives, body(): structure_factor = lax.psum(factor_part, ('row', 'col'))  148 us
    psum x1, waiting for transfers between devices, broadcast(): return lax.psum(jnp.where(mine, array, jnp.zeros_like(array)), axis)  77.2 us
    all_to_all x1, blocking collectives, body(): lax.all_to_all(dressed_cols, 'depth', split_axis=1, concat_axis=0, tiled=...  74.7 us
    unnamed x5, waiting for transfers between devices  42.4 us
    all_gather x1, blocking collectives, body(): vertex_rows = lax.all_gather(coulomb_vertex, 'col', axis=1, tiled=True)  33.1 us
  transfers between devices with their start and end apart: 4, of which 3 were waited for; matrix products, arithmetic and copies ran while one was open for 0% of the time, Pallas kernels for 0%

commit v1 on v0

--- a/solution.py
+++ b/solution.py
@@ -14,7 +14,9 @@
     col_index = lax.axis_index("col")
     block_width = amplitudes.shape[0]
     on_diagonal = (row_index == col_index).astype(jnp.float32)
-    vertex_rows = lax.all_gather(coulomb_vertex, "col", axis=1, tiled=True)
+    vertex_rows = jnp.concatenate(
+        lax.all_to_all(jnp.stack([coulomb_vertex] * lax.axis_size("col")), "col", 0, 0), axis=1
+    )
     vertex_cols = broadcast(vertex_rows, "row", col_index)
     dressing = jnp.dot(vertex_rows, amplitudes, preferred_element_type=jnp.float32)
     factor_part = jnp.sum(dressing * vertex_cols.astype(jnp.float32), axis=1)

time: 712 us -> 693 us (0.973)
  blocking collectives: 256 us -> 223 us
  starting transfers between devices: 0.16 us -> 8.66 us
    all_gather x1 -> x0, blocking collectives: 33.1 us -> none  [body(): vertex_rows = lax.all_gather(coulomb_vertex, 'col', axis=1, tiled=True)]
    all_to_all x0 -> x1, waiting for transfers between devices: none -> 11.7 us  [body(): lax.all_to_all(jnp.stack([coulomb_vertex] * lax.axis_size('col')), 'col',...]
    all_to_all x0 -> x1, starting transfers between devices: none -> 8.49 us  [body(): lax.all_to_all(jnp.stack([coulomb_vertex] * lax.axis_size('col')), 'col',...]
    psum x1, waiting for transfers between devices: 77.2 us -> 68.8 us  [broadcast(): return lax.psum(jnp.where(mine, array, jnp.zeros_like(array)), axis)]
  transfers between devices with their start and end apart: 4 -> 5, of which waited for: 3 -> 4; matrix products, arithmetic and copies ran while one was open for 0% -> 0% of each run, Pallas kernels for 0% -> 0%
where the time goes in v1:
time: 693 us; the launch traced here: 692 us
  waiting for transfers between devices  424 us (61%)
  blocking collectives  223 us (32%)
  between operations  13.8 us (2%)
  matrix products  12.9 us (2%)
  starting transfers between devices  8.66 us (1%)
  local copies, waits for them, and re-layouts  7.63 us (1%)
    all_gather x1, waiting for transfers between devices, body(): everything = lax.all_gather(dressed, ('row', 'col'), axis=1, tiled=True)  301 us
    psum x1, blocking collectives, body(): structure_factor = lax.psum(factor_part, ('row', 'col'))  148 us
    all_to_all x1, blocking collectives, body(): lax.all_to_all(dressed_cols, 'depth', split_axis=1, concat_axis=0, tiled=...  74.7 us
    psum x1, waiting for transfers between devices, broadcast(): return lax.psum(jnp.where(mine, array, jnp.zeros_like(array)), axis)  68.8 us
    unnamed x5, waiting for transfers between devices  42.3 us
  transfers between devices with their start and end apart: 5, of which 4 were waited for; matrix products, arithmetic and copies ran while one was open for 0% of the time, Pallas kernels for 0%

profile of v1, /device:TPU:1, one launch (start us, length us, event | category | flops | bytes accessed | tf_op | source)
XLA Modules:
  0.0 692.2 jit_solution(9735793142225674518)
XLA Ops:
  7.2 1.8 stack.2
  9.0 8.5 %all-to-all-start = ((bf16[8,128,320]{1,2,0:T(8,128)(2,1)}), bf16[8,128,320]{1,2,0:T(8,128)(2,1)S(1)}, u32[]{:S(2)}, u32[]{:S(2)}) async-start(bf16[8,128,320]{1,2,0:T(8,128)(2,1)} %stack.2), calls=%async_computation | async-start | bytes 1310720 | tf_op jit(solution)/shard_map/all_to_all | solution.py:18
  17.5 0.0 all-reduce.2.cloned.1.call-start
  17.5 11.7 %all-to-all-done = bf16[8,128,320]{1,2,0:T(8,128)(2,1)S(1)} async-done(((bf16[8,128,320]{1,2,0:T(8,128)(2,1)}), bf16[8,128,320]{1,2,0:T(8,128)(2,1)S(1)}, u32[]{:S(2)}, u32[]{:S(2)}) %all-to-all-start) | async-done | bytes 655392 | tf_op jit(solution)/shard_map/all_to_all | solution.py:18
  29.3 0.2 copy.19
  29.5 0.9 broadcast_select_fusion
  30.4 0.0 all-reduce.2.cloned.1.call-update
  30.4 0.0 reduce-scatter.4.cloned.1.call-start
  30.5 68.8 %all-reduce.2.cloned.1.call-done = bf16[128,2560]{1,0:T(8,128)(2,1)} async-done(((bf16[128,2560]{1,0:T(8,128)(2,1)}), bf16[128,2560]{1,0:T(8,128)(2,1)}) %all-reduce.2.cloned.1.call-update) | async-done | bytes 655376 | tf_op jit(solution)/shard_map/psum | solution.py:9
  99.3 6.9 multiply_reduce_fusion
  106.2 1.5 copy.24
  107.6 0.0 reduce-scatter.4.cloned.1.call-update
  107.6 0.0 all-gather.3.cloned.1.call-start
  107.7 42.3 %reduce-scatter.4.cloned.1.call-done = f32[320,128]{1,0:T(8,128)} async-done(((f32[2560,128]{1,0:T(8,128)}), f32[320,128]{1,0:T(8,128)}) %reduce-scatter.4.cloned.1.call-update) | async-done | bytes 163856
  150.0 1.6 bitcast_convert_fusion
  151.5 0.0 all-gather.3.cloned.1.call-update
  151.5 0.0 all-gather.5.cloned.1.call-start
  151.6 300.9 %all-gather.3.cloned.1.call-done = bf16[128,20480]{0,1:T(8,128)(2,1)} async-done(((bf16[128,320]{0,1:T(8,128)(2,1)}), bf16[128,20480]{0,1:T(8,128)(2,1)}) %all-gather.3.cloned.1.call-update) | async-done | bytes 5242896 | tf_op jit(solution)/shard_map/all_gather | solution.py:27
  452.5 2.9 copy.21
  455.5 0.9 constant_dynamic-slice_fusion
  456.4 0.0 all-gather.5.cloned.1.call-update
  456.4 148.3 %psum.15 = f32[128]{0:T(128)} all-reduce(f32[128]{0:T(128)S(1)} %get-tuple-element.4), channel_id=1, replica_groups=mesh['row'=8,'col'=8,'depth'=2] {'row','col'}, use_global_device_ids=true, to_apply=%region_3.4 | all-reduce | flops 128 | bytes 1024 | tf_op jit(solution)/shard_map/psum | solution.py:23
  604.7 74.7 %all_to_all.24 = bf16[128,2,1280]{0,2,1:T(8,128)(2,1)S(1)} all-to-all(bf16[128,2,1280]{0,2,1:T(8,128)(2,1)S(1)} %bitcast.24), channel_id=1, replica_groups=mesh['row'=8,'col'=8,'depth'=2] {'depth'}, dimensions={1} | all-to-all | bytes 1310720 | tf_op jit(solution)/shard_map/all_to_all | solution.py:36
  679.4 0.2 copy.22
  679.7 0.0 all-gather.5.cloned.1.call-done
  679.7 6.0 convolution_convert_fusion
Async XLA Ops:
  9.0 20.3 %all-to-all-start = ((bf16[8,128,320]{1,2,0:T(8,128)(2,1)}), bf16[8,128,320]{1,2,0:T(8,128)(2,1)S(1)}, u32[]{:S(2)}, u32[]{:S(2)}) async-start(bf16[8,128,320]{1,2,0:T(8,128)(2,1)} %stack.2), calls=%async_computation | async-start | bytes 1310720 | tf_op jit(solution)/shard_map/all_to_all | solution.py:18
  17.5 81.8 %all-reduce.2.cloned.1.call-start = ((), (), s32[]{:S(2)}) async-start(), calls=%async_computation.5 | async-start | bytes 1310720 | tf_op jit(solution)/shard_map/psum | solution.py:9
  30.4 119.5 %reduce-scatter.4.cloned.1.call-start = ((), (), s32[]{:S(2)}) async-start(), calls=%async_computation.6 | async-start | bytes 1474560
  107.6 344.9 %all-gather.3.cloned.1.call-start = ((), (), s32[]{:S(2)}) async-start(), calls=%async_computation.3 | async-start | bytes 5324800 | tf_op jit(solution)/shard_map/all_gather | solution.py:27
  151.5 528.2 %all-gather.5.cloned.1.call-start = ((), (), s32[]{:S(2)}) async-start(), calls=%async_computation.4 | async-start | bytes 1966080 | tf_op jit(solution)/shard_map/all_gather | solution.py:37
Sparse Core Ops, SparseCore 0:
  30.5 68.6 all-reduce.1
  107.8 42.1 reduce-scatter.3
  152.2 300.3 all-gather.2
  456.5 51.9 all-gather.4

commit v2 on v0

--- a/solution.py
+++ b/solution.py
@@ -18,7 +18,7 @@
     vertex_cols = broadcast(vertex_rows, "row", col_index)
     dressing = jnp.dot(vertex_rows, amplitudes, preferred_element_type=jnp.float32)
     factor_part = jnp.sum(dressing * vertex_cols.astype(jnp.float32), axis=1)
-    structure_factor = lax.psum(factor_part, ("row", "col"))
+    structure_factor = lax.psum(lax.psum(factor_part, "row"), "col")
     dressed_term = dressing + on_diagonal * vertex_rows.astype(jnp.float32)
     dressed_part = lax.psum_scatter(dressed_term, "row", scatter_dimension=1, tiled=True)
     dressed = dressed_part.astype(jnp.bfloat16)

time: 712 us -> 577 us (0.81)
  blocking collectives: 256 us -> 121 us
    psum x1 -> x2, blocking collectives: 148 us -> 33.4 us  [body(): structure_factor = lax.psum(lax.psum(factor_part, 'row'), 'col')]
    all_to_all x1, blocking collectives: 74.7 us -> 54.2 us  [body(): lax.all_to_all(dressed_cols, 'depth', split_axis=1, concat_axis=0, tiled=...]
where the time goes in v2:
time: 577 us
  waiting for transfers between devices  421 us (73%)
  blocking collectives  121 us (21%)
  between operations  13.8 us (2%)
  matrix products  12.9 us (2%)
  local copies, waits for them, and re-layouts  5.82 us (1%)
    all_gather x1, waiting for transfers between devices, body(): everything = lax.all_gather(dressed, ('row', 'col'), axis=1, tiled=True)  301 us
    psum x1, waiting for transfers between devices, broadcast(): return lax.psum(jnp.where(mine, array, jnp.zeros_like(array)), axis)  77.2 us
    all_to_all x1, blocking collectives, body(): lax.all_to_all(dressed_cols, 'depth', split_axis=1, concat_axis=0, tiled=...  54.2 us
    unnamed x5, waiting for transfers between devices  42.4 us
    psum x2, blocking collectives, body(): structure_factor = lax.psum(lax.psum(factor_part, 'row'), 'col')  33.4 us
    all_gather x1, blocking collectives, body(): vertex_rows = lax.all_gather(coulomb_vertex, 'col', axis=1, tiled=True)  33.1 us
  transfers between devices with their start and end apart: 4, of which 3 were waited for; matrix products, arithmetic and copies ran while one was open for 0% of the time, Pallas kernels for 0%

profile of v2, /device:TPU:1, one launch (start us, length us, event | category | flops | bytes accessed | tf_op | source)
XLA Modules:
  0.0 576.5 jit_solution(13179857993816247356)
XLA Ops:
  7.2 0.0 all-reduce.2.cloned.1.call-start
  7.2 33.1 %all_gather.9 = bf16[128,2560]{0,1:T(8,128)(2,1)S(1)} all-gather(bf16[128,320]{0,1:T(8,128)(2,1)} %param.3), channel_id=1, replica_groups=mesh['row'=8,'col'=8,'depth'=2] {'col'}, dimensions={1}, use_global_device_ids=true | all-gather | bytes 737280 | tf_op jit(solution)/shard_map/all_gather | solution.py:17
  40.3 0.2 copy.17
  40.6 0.9 broadcast_select_fusion
  41.5 0.0 all-reduce.2.cloned.1.call-update
  41.5 0.0 reduce-scatter.4.cloned.1.call-start
  41.5 77.2 %all-reduce.2.cloned.1.call-done = bf16[128,2560]{1,0:T(8,128)(2,1)} async-done(((bf16[128,2560]{1,0:T(8,128)(2,1)}), bf16[128,2560]{1,0:T(8,128)(2,1)}) %all-reduce.2.cloned.1.call-update) | async-done | bytes 655376 | tf_op jit(solution)/shard_map/psum | solution.py:9
  118.7 6.9 %multiply_reduce_fusion = (f32[128]{0:T(128)S(1)}, f32[128,2560]{1,0:T(8,128)S(1)}) fusion(bf16[128,2560]{1,0:T(8,128)(2,1)} %all-reduce.2.cloned.1.call-done, bf16[128,2560]{1,0:T(8,128)(2,1)S(1)} %copy.17, f32[]{:T(128)S(6)} %convert_element_type.15, bf16[128,2560]{0,1:T(8,128)(2,1)S(1)} %all_gather.9, bf16[2560,2560]{1,0:T(8,128)(2,1)} %param.2), kind=kOutput, calls=%fused_computation.1 | convolution fusion | flops 1679687552 | bytes 16384516 | tf_op jit(solution)/shard_map/dot_general | solution.py:19
  125.6 1.5 copy.22
  127.1 0.0 reduce-scatter.4.cloned.1.call-update
  127.1 0.0 all-gather.3.cloned.1.call-start
  127.1 42.3 %reduce-scatter.4.cloned.1.call-done = f32[320,128]{1,0:T(8,128)} async-done(((f32[2560,128]{1,0:T(8,128)}), f32[320,128]{1,0:T(8,128)}) %reduce-scatter.4.cloned.1.call-update) | async-done | bytes 163856
  169.5 1.6 bitcast_convert_fusion
  171.0 0.0 all-gather.3.cloned.1.call-update
  171.1 0.0 all-gather.5.cloned.1.call-start
  171.1 301.0 %all-gather.3.cloned.1.call-done = bf16[128,20480]{0,1:T(8,128)(2,1)} async-done(((bf16[128,320]{0,1:T(8,128)(2,1)}), bf16[128,20480]{0,1:T(8,128)(2,1)}) %all-gather.3.cloned.1.call-update) | async-done | bytes 5242896 | tf_op jit(solution)/shard_map/all_gather | solution.py:25
  472.2 2.9 copy.19
  475.1 0.9 constant_dynamic-slice_fusion
  476.0 0.0 all-gather.5.cloned.1.call-update
  476.1 13.7 %psum.22 = f32[128]{0:T(128)S(1)} all-reduce(f32[128]{0:T(128)S(1)} %get-tuple-element.4), channel_id=1, replica_groups=mesh['row'=8,'col'=8,'depth'=2] {'row'}, use_global_device_ids=true, to_apply=%region_3.4 | all-reduce | flops 128 | bytes 1024 | tf_op jit(solution)/shard_map/psum | solution.py:21
  489.7 19.8 %psum.23 = f32[128]{0:T(128)} all-reduce(f32[128]{0:T(128)S(1)} %psum.22), channel_id=1, replica_groups=mesh['row'=8,'col'=8,'depth'=2] {'col'}, use_global_device_ids=true, to_apply=%region_4.5 | all-reduce | flops 128 | bytes 1024 | tf_op jit(solution)/shard_map/psum | solution.py:21
  509.5 54.2 %all_to_all.19 = bf16[128,2,1280]{0,2,1:T(8,128)(2,1)S(1)} all-to-all(bf16[128,2,1280]{0,2,1:T(8,128)(2,1)S(1)} %bitcast.19), channel_id=1, replica_groups=mesh['row'=8,'col'=8,'depth'=2] {'depth'}, dimensions={1} | all-to-all | bytes 1310720 | tf_op jit(solution)/shard_map/all_to_all | solution.py:34
  563.7 0.2 copy.20
  564.0 0.0 all-gather.5.cloned.1.call-done
  564.0 6.0 %convolution_convert_fusion = bf16[2560,1280]{1,0:T(8,128)(2,1)} fusion(bf16[256,2560]{0,1:T(8,128)(2,1)} %all-gather.5.cloned.1.call-done, bf16[256,1280]{1,0:T(8,128)(2,1)S(1)} %bitcast.17), kind=kOutput, calls=%fused_computation | convolution fusion | flops 1680998400 | bytes 8519680 | tf_op jit(solution)/shard_map/dot_general | solution.py:36
Async XLA Ops:
  7.2 111.5 %all-reduce.2.cloned.1.call-start = ((), (), s32[]{:S(2)}) async-start(), calls=%async_computation.4 | async-start | bytes 1310720 | tf_op jit(solution)/shard_map/psum | solution.py:9
  41.5 128.0 %reduce-scatter.4.cloned.1.call-start = ((), (), s32[]{:S(2)}) async-start(), calls=%async_computation.5 | async-start | bytes 1474560
  127.1 345.1 %all-gather.3.cloned.1.call-start = ((), (), s32[]{:S(2)}) async-start(), calls=%async_computation.2 | async-start | bytes 5324800 | tf_op jit(solution)/shard_map/all_gather | solution.py:25
  171.1 393.0 %all-gather.5.cloned.1.call-start = ((), (), s32[]{:S(2)}) async-start(), calls=%async_computation.3 | async-start | bytes 1966080 | tf_op jit(solution)/shard_map/all_gather | solution.py:35
Sparse Core Ops, SparseCore 0:
  41.6 77.0 all-reduce.1
  127.2 42.2 reduce-scatter.3
  171.7 300.4 all-gather.2
  476.2 51.8 all-gather.4
